TPU v7x, 512 devices: a whole 4x8x8 slice. The times are simulated.
512 devices in a mesh: member: 2 (over core), fsdp: 256 (over y, x, z).
Axes of the slice: x: 4, y: 8, z: 8, core: 2. Of those that a mesh axis runs over, the one named last changes fastest.
Arguments:
- hidden: bfloat16 [2, 512, 2048], P('member', 'fsdp'), may hold values from -60 to 60
- gain: float32 [2, 2048], P('member'), may hold values from 0.5 to 1.5
- head: bfloat16 [2, 2048, 128256], P('member', None, 'fsdp'), may hold values from -0.397747564 to 0.397747564
- labels: int32 [512], replicated, may hold values from 0 to 128255
Outputs:
- token_loss: float32 [2, 512], P('member', 'fsdp')
- head_grad: bfloat16 [2, 2048, 128256], P('member', None, 'fsdp')
- hidden_grad: bfloat16 [2, 512, 2048], P('member', 'fsdp')
All inputs are finite; a program needn't handle non-finite values.
Results may differ from a plain program's by a relative error of at most 0.0049.
Values may be sent and summed in bfloat16 or wider, within the bound.
A program may use at most 64 MiB of HBM per device.

v0:
```python
import jax
import jax.numpy as jnp
from jax import lax
from jax.sharding import PartitionSpec as P

EPS = 1e-05
BETA = 0.5


def swapped(value, axis, bit):
    return lax.ppermute(value, axis, [(i, i ^ 1 << bit) for i in range(lax.axis_size(axis))])


def normalize(rows, gain_row):
    values = rows.astype(jnp.float32)
    inverse = lax.rsqrt(jnp.mean(values * values, axis=-1, keepdims=True) + EPS)
    return ((values * inverse * gain_row).astype(jnp.bfloat16), inverse)


def norm_back(rows, inverse, gain_row, upstream):
    values = rows.astype(jnp.float32)
    scaled = gain_row * upstream
    inner = jnp.mean(scaled * values, axis=-1, keepdims=True)
    return inverse * scaled - values * inverse**3 * inner


def body(hidden, gain, head, labels):
    own_rows = hidden[0]
    gain_row = gain[0]
    weights_local = head[0]
    tok_dev = own_rows.shape[0]
    vocab_dev = weights_local.shape[1]
    own_start = lax.axis_index("fsdp") * tok_dev
    vocab_start = lax.axis_index("fsdp") * vocab_dev
    normed_own, inverse_own = normalize(own_rows, gain_row)
    normed = lax.all_gather(normed_own, "fsdp", axis=0, tiled=True)
    token_count = normed.shape[0]
    logits = jnp.dot(normed, weights_local, preferred_element_type=jnp.float32)
    local_label = labels - vocab_start
    columns = lax.broadcasted_iota(jnp.int32, (1, vocab_dev), 1)
    onehot_mask = local_label[:, None] == columns
    picked_part = jnp.sum(jnp.where(onehot_mask, logits, 0.0), axis=-1)
    row_top = lax.pmax(jnp.max(logits, axis=-1), "fsdp")
    row_total, picked = lax.psum(
        (jnp.sum(jnp.exp(logits - row_top[:, None]), axis=-1), picked_part), "fsdp"
    )
    log_total = row_top + jnp.log(row_total)
    logprob = (logits - log_total[:, None]).astype(jnp.bfloat16)
    teacher = swapped(logprob, "member", 0)
    target = jnp.exp(teacher.astype(jnp.float32))
    student = jnp.exp(logits - log_total[:, None])
    dlogits = (
        ((1.0 + BETA) * student - onehot_mask.astype(jnp.float32) - BETA * target) / token_count
    ).astype(jnp.bfloat16)
    cross_part = jnp.sum(target * (log_total[:, None] - logits), axis=-1)
    head_grad = lax.dot_general(
        normed, dlogits, (((0,), (0,)), ((), ())), preferred_element_type=jnp.float32
    ).astype(jnp.bfloat16)
    cross_whole = lax.psum(cross_part, "fsdp")
    cross_own = lax.dynamic_slice_in_dim(cross_whole, own_start, tok_dev, 0)
    partial_up = lax.dot_general(
        dlogits, weights_local, (((1,), (1,)), ((), ())), preferred_element_type=jnp.float32
    )
    summed = lax.psum_scatter(partial_up, "fsdp", scatter_dimension=0, tiled=True)
    total_own = lax.dynamic_slice_in_dim(log_total, own_start, tok_dev, 0)
    picked_own = lax.dynamic_slice_in_dim(picked, own_start, tok_dev, 0)
    token_loss = total_own - picked_own + BETA * cross_own
    hidden_grad = norm_back(own_rows, inverse_own, gain_row, summed)
    return (token_loss[None], head_grad[None], hidden_grad.astype(jnp.bfloat16)[None])


def solution(mesh):
    in_specs = (P("member", "fsdp", None), P("member", None), P("member", None, "fsdp"), P())
    out_specs = (P("member", "fsdp"), P("member", None, "fsdp"), P("member", "fsdp", None))
    return jax.shard_map(body, mesh=mesh, in_specs=in_specs, out_specs=out_specs, check_vma=False)
```

profile of v0, /device:TPU:64, one launch (start us, length us, event | category | flops | bytes accessed | tf_op | source)
XLA Modules:
  0.0 2222.8 jit_solution(17684733254813426398)
XLA Ops:
  7.2 0.0 copy-start
  7.2 0.0 all-gather.3.cloned.1.call-start
  7.2 1.0 fusion.5
  8.2 1.4 fusion.12
  9.6 0.0 all-gather.3.cloned.1.call-update
  9.6 0.0 all-reduce.4.cloned.1.call-start
  9.7 123.2 %all-gather.3.cloned.1.call-done = bf16[256,2,2048]{2,1,0:T(2,128)(2,1)} async-done(((bf16[1,2,2048]{2,1,0:T(2,128)(2,1)}), bf16[256,2,2048]{2,1,0:T(2,128)(2,1)}) %all-gather.3.cloned.1.call-update) | async-done | bytes 2097168 | tf_op jit(solution)/shard_map/all_gather | solution.py:36
  132.8 4.1 reshape.31
  137.0 0.0 copy-done
  137.0 2.9 fusion.14
  139.9 0.0 copy-start.5
  139.9 683.9 %pmax.7 = f32[512]{0:T(512)S(1)} all-reduce(f32[512]{0:T(512)S(1)} %get-tuple-element.10), channel_id=1, replica_groups=mesh['member'=2,'fsdp'=256] {'fsdp'}, use_global_device_ids=true, to_apply=%region_2.3 | all-reduce | flops 512 | bytes 4096 | tf_op jit(solution)/shard_map/pmax | solution.py:43
  823.8 0.2 exponential_reduce_fusion
  824.0 688.2 %psum.21 = f32[512]{0:T(512)S(1)} all-reduce(f32[512]{0:T(512)S(1)} %exponential_reduce_fusion), channel_id=1, replica_groups=mesh['member'=2,'fsdp'=256] {'fsdp'}, use_global_device_ids=true, to_apply=%region_4.5 | all-reduce | flops 512 | bytes 4096 | tf_op jit(solution)/shard_map/psum | solution.py:44
  1512.2 0.9 subtract_convert_fusion
  1513.1 1.9 collective-permute-start
  1515.0 0.0 copy-done.5
  1515.1 2.2 collective-permute-done
  1517.3 1.7 select_reduce_fusion
  1519.0 0.0 copy-start.1
  1519.0 0.8 copy-done.1
  1519.8 3.3 fusion.1
  1523.0 0.0 all-reduce.4.cloned.1.call-update
  1523.1 1.3 dynamic-slice
  1525.0 683.7 %all-reduce.1 = (f32[512]{0:T(512)S(1)}, f32[512]{0:T(512)S(1)}) all-reduce(f32[512]{0:T(512)S(1)} %get-tuple-element.4, f32[512]{0:T(512)S(1)} %get-tuple-element.3), channel_id=1, replica_groups=mesh['member'=2,'fsdp'=256] {'fsdp'}, use_global_device_ids=true, to_apply=%region_8.9 | all-reduce | flops 1024 | bytes 8192 | tf_op jit(solution)/shard_map/psum | solution.py:59
  2208.7 0.6 add_bitcast_fusion
  2209.3 0.0 copy-done.2
  2209.3 4.2 fusion
  2213.4 0.0 copy-done.3
  2213.5 0.0 copy-done.4
  2213.5 1.0 fusion.11
  2214.4 1.5 fusion.13
  (8 shorter events, 0.0 us)
Async XLA Ops:
  7.2 129.8 %copy-start = (bf16[1,2048,501]{1,2,0:T(8,128)(2,1)S(1)}, bf16[1,2048,501]{1,2,0:T(8,128)(2,1)}, u32[]{:S(2)}) copy-start(bf16[1,2048,501]{1,2,0:T(8,128)(2,1)} %param.6) | copy-start | bytes 6156292
  7.2 125.7 %all-gather.3.cloned.1.call-start = ((), (), s32[]{:S(2)}) async-start(), calls=%async_computation | async-start | bytes 2105344 | tf_op jit(solution)/shard_map/all_gather | solution.py:36
  9.6 2203.8 %all-reduce.4.cloned.1.call-start = ((), (), s32[]{:S(2)}) async-start(), calls=%async_computation.1 | async-start | bytes 8388608
  139.9 1375.2 %copy-start.5 = (s32[512]{0:T(512)S(1)}, s32[512]{0:T(512)}, u32[]{:S(2)}) copy-start(s32[512]{0:T(512)} %param.7) | copy-start | bytes 6148
  1513.1 4.1 collective-permute-start
  1519.0 0.8 copy-start.1
  1523.0 686.3 %copy-start.2 = (bf16[512,501]{0,1:T(8,128)(2,1)S(1)}, bf16[512,501]{0,1:T(8,128)(2,1)}, u32[]{:S(2)}) copy-start(bf16[512,501]{0,1:T(8,128)(2,1)} %copy-done.1) | copy-start | bytes 1539076
  2209.3 4.2 copy-start.3
  2209.3 4.2 copy-start.4
Sparse Core Ops, SparseCore 0:
  12.6 120.1 all-gather.2
  1523.2 244.8 all-reduce.3
where the time goes:
time: 2220 us
  blocking collectives  2060 us (93%)
  waiting for transfers between devices  125 us (6%)
    psum x1, blocking collectives, body(): lax.psum((jnp.sum(jnp.exp(logits - row_top[:, None]), axis=-1), picked_pa...  688 us
    pmax x1, blocking collectives, body(): row_top = lax.pmax(jnp.max(logits, axis=-1), 'fsdp')  684 us
    psum x1, blocking collectives, body(): cross_whole = lax.psum(cross_part, 'fsdp')  684 us
    all_gather x1, waiting for transfers between devices, body(): normed = lax.all_gather(normed_own, 'fsdp', axis=0, tiled=True)  123 us
  transfers between devices with their start and end apart: 3, of which 2 were waited for; matrix products, arithmetic and copies ran while one was open for 0% of the time, Pallas kernels for 0%

commit v1 on v0

v1 whole, which is shorter than its diff:
```python
import functools
import math

import jax
import jax.numpy as jnp
from jax import lax
from jax.experimental import pallas as pl
from jax.experimental.pallas import tpu as pltpu
from jax.sharding import PartitionSpec as P

EPS = 1e-05
BETA = 0.5
MESH = pl.DeviceIdType.MESH
F32 = jnp.float32
BF16 = jnp.bfloat16
GRID = {256: (8, 4, 8), 8: (2, 2, 2)}
SPLIT = {2048: (384, 1024, 640), 384: (128, 128, 128)}

G1Z, G1Y, G2A, G2B, G2C, G3A, G3B, G3C = range(8)
SZ, SY, SX, TE = range(8, 12)
R1A, R1B, R1C, R2A, R2B, R2C, R3Z, R3Y = range(12, 20)
QX, QY, QZ = range(20, 23)
NEX = 23


def dot(a, b, dims):
    return lax.dot_general(a, b, (dims, ((), ())), preferred_element_type=F32)


def kernel(
    dims, parts, hid, gain, head_hbm, lab, loss, hg_hbm, hd,
    w, own, z1, y1, asz, asy, na, nc, nb, nbn, lg, tch, stz, sty, stx, ltt, labt,
    dl, dlb, ua, uc, ub, ra, rc, rb, sa2, sc2, sb2, ra2, rc2, rb2,
    s3z, s3y, r3z, r3y, qz, qy, qx, hg, ssem, rsem, csem,
):
    ny, nx, nz = dims
    fa, fc, fb = parts
    fac = fa + fc
    rows, feat = hid.shape
    tokens = lab.shape[1]
    vocab = head_hbm.shape[1]
    gz, gy = nz * rows, ny * rows

    f = lax.axis_index("fsdp")
    mem = lax.axis_index("member")
    z = lax.rem(f, nz)
    x = lax.rem(lax.div(f, nz), nx)
    y = lax.div(f, nz * nx)

    def at_z(c):
        return {"fsdp": f - z + c}

    def at_x(c):
        return {"fsdp": f + (c - x) * nz}

    def at_y(c):
        return {"fsdp": f + (c - y) * (nx * nz)}

    def copy(num, k, src, dst, dev):
        return pltpu.make_async_remote_copy(
            src_ref=src, dst_ref=dst, send_sem=ssem.at[num, k], recv_sem=rsem.at[num, k],
            device_id=dev, device_id_type=MESH,
        )

    sends = []

    class Exchange:
        def __init__(self, num, n, me, at, src, dst):
            self.n = n

            def make(k):
                c = lax.rem(me + k, n)
                return copy(num, k, src(c), dst, at(c))

            self.make = make
            sends.append(self)

        def each(self, do):
            def step(k, carry):
                do(self.make(k))
                return carry

            lax.fori_loop(1, self.n, step, 0)

        def start(self):
            self.each(lambda c: c.start())
            return self

        def arrived(self):
            self.each(lambda c: c.wait_recv())

        def sent(self):
            self.each(lambda c: c.wait_send())

    load = pltpu.make_async_copy(head_hbm, w, csem.at[0])
    load.start()

    barrier = pltpu.get_barrier_semaphore()

    def greet(dev):
        pl.semaphore_signal(barrier, inc=1, device_id=dev, device_id_type=MESH)

    def greet_all(n, me, at):
        def step(k, carry):
            greet(at(lax.rem(me + k, n)))
            return carry

        lax.fori_loop(1, n, step, 0)

    greet_all(nz, z, at_z)
    greet_all(ny, y, at_y)
    greet_all(nx, x, at_x)
    def at_x_other(c):
        return {"member": 1 - mem, "fsdp": f + (c - x) * nz}

    def greet_other(c, carry):
        greet(at_x_other(c))
        return carry

    lax.fori_loop(0, nx, greet_other, 0)

    values = hid[...].astype(F32)
    inverse = lax.rsqrt(jnp.mean(values * values, axis=-1, keepdims=True) + EPS)
    own[...] = (values * inverse * gain[...]).astype(BF16)

    pl.semaphore_wait(barrier, nz - 1 + ny - 1 + nx - 1 + nx)

    g1y = Exchange(G1Y, ny, y, at_y, lambda c: own.at[:, pl.ds(fac, fb)], y1.at[y]).start()
    g1z = Exchange(G1Z, nz, z, at_z, lambda c: own.at[:, pl.ds(0, fac)], z1.at[z]).start()

    z1[z] = own[:, :fac]
    y1[y] = own[:, fac:]
    labt[...] = jnp.broadcast_to(lab[...], (128, tokens)).T
    size = ny * gz
    lr = int(math.log2(rows))
    lz = int(math.log2(nz))
    to = lax.broadcasted_iota(jnp.int32, (size, size), 0)
    frm = lax.broadcasted_iota(jnp.int32, (size, size), 1)
    ty = to >> (lr + lz)
    tz = (to >> lr) & (nz - 1)
    perm = (frm == tz * gy + ty * rows + (to & (rows - 1))).astype(BF16)

    g1y.arrived()
    for s in range(ny):
        asy[s * rows:(s + 1) * rows, :] = y1[s].astype(F32)
    nb[x, z] = asy[...].astype(BF16)
    g2b = Exchange(G2B, nx, x, at_x, lambda c: nb.at[x, z], nb.at[x, z]).start()
    g1z.arrived()
    for s in range(nz):
        asz[s * rows:(s + 1) * rows, :] = z1[s].astype(F32)
    tile = asz[...].astype(BF16)
    na[y, x] = tile[:, :fa]
    nc[y, x] = tile[:, fa:]
    g2a = Exchange(G2A, nx, x, at_x, lambda c: na.at[y, x], na.at[y, x]).start()
    g2c = Exchange(G2C, ny, y, at_y, lambda c: nc.at[y, x], nc.at[y, x]).start()
    g2b.arrived()
    g3b = Exchange(G3B, nz, z, at_z, lambda c: nb.at[:, z], nb.at[:, z]).start()
    g2a.arrived()
    g3a = Exchange(G3A, ny, y, at_y, lambda c: na.at[y], na.at[y]).start()
    g2c.arrived()
    g3c = Exchange(G3C, nx, x, at_x, lambda c: nc.at[:, x], nc.at[:, x]).start()

    load.wait()
    g3c.arrived()
    lg[...] = dot(nc[...].reshape(tokens, fc), w[fa:fac, :], ((1,), (0,)))
    g3a.arrived()
    lg[...] += dot(na[...].reshape(tokens, fa), w[:fa, :], ((1,), (0,)))
    g3b.arrived()
    for s in range(nx):
        swap = dot(perm, nb[s].reshape(size, fb), ((1,), (0,)))
        nbn[:, s] = swap.astype(BF16).reshape(ny, gz, fb)
    lg[...] += dot(nbn[...].reshape(tokens, fb), w[fac:, :], ((1,), (0,)))
    other = copy(TE, 0, lg, tch, {"member": 1 - mem})
    other.start()

    logits = lg[...]
    columns = lax.broadcasted_iota(jnp.int32, (tokens, vocab), 1)
    top = jnp.max(logits, axis=-1, keepdims=True)
    total = jnp.sum(jnp.exp(logits - top), axis=-1, keepdims=True)
    lane = lax.broadcasted_iota(jnp.int32, (tokens, 128), 1)
    both = jnp.where(lane == 0, top, total).T
    stz[z] = both[0:2, :]

    def merged(blocks):
        best = functools.reduce(jnp.maximum, [b[0:1, :] for b in blocks])
        return best, functools.reduce(jnp.add, [b[1:2, :] * jnp.exp(b[0:1, :] - best) for b in blocks])

    sz = Exchange(SZ, nz, z, at_z, lambda c: stz.at[z], stz.at[z]).start()
    sz.arrived()
    best, total = merged([stz[s] for s in range(nz)])
    sty[y, 0:1, :] = best
    sty[y, 1:2, :] = total
    sy = Exchange(SY, ny, y, at_y, lambda c: sty.at[y], sty.at[y]).start()
    sy.arrived()
    best, total = merged([sty[s] for s in range(ny)])
    stx[mem, x, 0:1, :] = best
    stx[mem, x, 1:2, :] = total

    sx = Exchange(SX, nx, x, at_x, lambda c: stx.at[mem, x], stx.at[mem, x]).start()

    def cross_copy(k):
        c = lax.rem(x + k, nx)
        return copy(SX, nx + k, stx.at[mem, x], stx.at[mem, x], at_x_other(c))

    def cross_each(do):
        def step(k, carry):
            do(cross_copy(k))
            return carry

        lax.fori_loop(0, nx, step, 0)

    cross_each(lambda c: c.start())
    sx.arrived()
    cross_each(lambda c: c.wait_recv())
    logs = []
    for who in (mem, 1 - mem):
        best, total = merged([stx[who, s] for s in range(nx)])
        logs.append(best + jnp.log(total))
    row = lax.broadcasted_iota(jnp.int32, (128, tokens), 0)
    ltt[...] = jnp.where(row == 0, logs[0], logs[1]).T

    other.wait_recv()
    local = labt[:, 0:1] - f * vocab
    mask = local == columns
    logits = lg[...]
    log_total = ltt[:, 0:1]
    target = jnp.exp((tch[...] - ltt[:, 1:2]).astype(BF16).astype(F32))
    student = jnp.exp(logits - log_total)
    grad = ((1.0 + BETA) * student - mask.astype(F32) - BETA * target) * (1.0 / tokens)
    dl[...] = grad.astype(BF16).reshape(ny, nx, gz, vocab)
    part = jnp.sum(BETA * target * (log_total - logits) - jnp.where(mask, logits, 0.0), axis=-1, keepdims=True)
    qx[x] = jnp.broadcast_to(part, (tokens, 128)).T[0:1, :]
    q1 = Exchange(QX, nx, x, at_x, lambda c: qx.at[x], qx.at[x]).start()

    for s in range(nx):
        swap = dot(perm, dl[:, s].reshape(size, vocab), ((0,), (0,)))
        dlb[s] = swap.astype(BF16).reshape(nz, gy, vocab)
    ub[...] = dot(dlb[...].reshape(tokens, vocab), w[fac:, :], ((1,), (1,))).astype(BF16).reshape(ub.shape)
    r1b = Exchange(R1B, nz, z, at_z, lambda c: ub.at[:, c], rb.at[z]).start()
    whole = dl[...].reshape(tokens, vocab)
    ua[...] = dot(whole, w[:fa, :], ((1,), (1,))).astype(BF16).reshape(ua.shape)
    r1a = Exchange(R1A, ny, y, at_y, lambda c: ua.at[c], ra.at[y]).start()
    uc[...] = dot(whole, w[fa:fac, :], ((1,), (1,))).astype(BF16).reshape(uc.shape)
    r1c = Exchange(R1C, nx, x, at_x, lambda c: uc.at[:, c], rc.at[x]).start()

    hg[:fa, :] = dot(na[...].reshape(tokens, fa), whole, ((0,), (0,))).astype(BF16)
    hg[fa:fac, :] = dot(nc[...].reshape(tokens, fc), whole, ((0,), (0,))).astype(BF16)
    hg[fac:, :] = dot(nbn[...].reshape(tokens, fb), whole, ((0,), (0,))).astype(BF16)
    store = pltpu.make_async_copy(hg, hg_hbm, csem.at[1])
    store.start()

    q1.arrived()
    qy[y] = functools.reduce(jnp.add, [qx[s] for s in range(nx)])
    q2 = Exchange(QY, ny, y, at_y, lambda c: qy.at[y], qy.at[y]).start()
    q2.arrived()
    qz[z] = functools.reduce(jnp.add, [qy[s] for s in range(ny)])
    q3 = Exchange(QZ, nz, z, at_z, lambda c: qz.at[z], qz.at[z]).start()

    def summed(mine, arrived, me, n, index):
        def step(k, acc):
            return acc + arrived[(lax.rem(me + k, n),) + index].astype(F32)

        acc = mine.astype(F32)
        for k in range(1, n):
            acc = step(k, acc)
        return acc

    r1c.arrived()
    for s in range(ny):
        sc2[s] = summed(uc[s, x], rc, x, nx, (s,)).astype(BF16)
    r2c = Exchange(R2C, ny, y, at_y, lambda c: sc2.at[c], rc2.at[y]).start()
    r1a.arrived()
    for s in range(nx):
        sa2[s] = summed(ua[y, s], ra, y, ny, (s,)).astype(BF16)
    r2a = Exchange(R2A, nx, x, at_x, lambda c: sa2.at[c], ra2.at[x]).start()
    r1b.arrived()
    for s in range(nx):
        sb2[s] = summed(ub[s, z], rb, z, nz, (s,)).astype(BF16)
    r2b = Exchange(R2B, nx, x, at_x, lambda c: sb2.at[c], rb2.at[x]).start()

    r2c.arrived()
    asz[:, fa:] = summed(sc2[y], rc2, y, ny, ())
    r2a.arrived()
    asz[:, :fa] = summed(sa2[x], ra2, x, nx, ())
    for s in range(nz):
        s3z[s] = asz[s * rows:(s + 1) * rows, :]
    r3 = Exchange(R3Z, nz, z, at_z, lambda c: s3z.at[c], r3z.at[z]).start()
    r2b.arrived()
    asy[...] = summed(sb2[x], rb2, x, nx, ())
    for s in range(ny):
        s3y[s] = asy[s * rows:(s + 1) * rows, :]
    r4 = Exchange(R3Y, ny, y, at_y, lambda c: s3y.at[c], r3y.at[y]).start()

    q3.arrived()
    losses = functools.reduce(jnp.add, [qz[s] for s in range(nz)]) + logs[0]
    spot = lax.broadcasted_iota(jnp.int32, (1, tokens), 1)
    for i in range(rows):
        loss[:, i:i + 1] = jnp.sum(jnp.where(spot == f * rows + i, losses, 0.0), axis=-1, keepdims=True)

    r3.arrived()
    r4.arrived()
    upstream = jnp.concatenate([summed(s3z[z], r3z, z, nz, ()), summed(s3y[y], r3y, y, ny, ())], axis=-1)
    scaled = gain[...] * upstream
    inner = jnp.mean(scaled * values, axis=-1, keepdims=True)
    hd[...] = (inverse * scaled - values * (inverse * inverse * inverse) * inner).astype(BF16)

    for exchange in sends:
        exchange.sent()
    cross_each(lambda c: c.wait_send())
    other.wait_send()
    store.wait()


def body(hidden, gain, head, labels):
    rows, feat = hidden.shape[1:]
    vocab = head.shape[2]
    tokens = labels.shape[0]
    ny, nx, nz = dims = GRID[tokens // rows]
    fa, fc, fb = parts = SPLIT[feat]
    fac = fa + fc
    gz, gy = nz * rows, ny * rows
    vm = pltpu.VMEM
    loss, head_grad, hidden_grad = pl.pallas_call(
        functools.partial(kernel, dims, parts),
        out_shape=(
            jax.ShapeDtypeStruct((1, rows), F32),
            jax.ShapeDtypeStruct((feat, vocab), BF16),
            jax.ShapeDtypeStruct((rows, feat), BF16),
        ),
        in_specs=[
            pl.BlockSpec(memory_space=vm),
            pl.BlockSpec(memory_space=vm),
            pl.BlockSpec(memory_space=pl.ANY),
            pl.BlockSpec(memory_space=vm),
        ],
        out_specs=(
            pl.BlockSpec(memory_space=vm),
            pl.BlockSpec(memory_space=pl.ANY),
            pl.BlockSpec(memory_space=vm),
        ),
        scratch_shapes=[
            vm((feat, vocab), BF16),
            vm((rows, feat), BF16),
            vm((nz, rows, fac), BF16),
            vm((ny, rows, fb), BF16),
            vm((gz, fac), F32),
            vm((gy, fb), F32),
            vm((ny, nx, gz, fa), BF16),
            vm((ny, nx, gz, fc), BF16),
            vm((nx, nz, gy, fb), BF16),
            vm((ny, nx, gz, fb), BF16),
            vm((tokens, vocab), F32),
            vm((tokens, vocab), F32),
            vm((nz, 2, tokens), F32),
            vm((ny, 2, tokens), F32),
            vm((2, nx, 2, tokens), F32),
            vm((tokens, 128), F32),
            vm((tokens, 128), jnp.int32),
            vm((ny, nx, gz, vocab), BF16),
            vm((nx, nz, gy, vocab), BF16),
            vm((ny, nx, gz, fa), BF16),
            vm((ny, nx, gz, fc), BF16),
            vm((nx, nz, gy, fb), BF16),
            vm((ny, nx, gz, fa), BF16),
            vm((nx, ny, gz, fc), BF16),
            vm((nz, nx, gy, fb), BF16),
            vm((nx, gz, fa), BF16),
            vm((ny, gz, fc), BF16),
            vm((nx, gy, fb), BF16),
            vm((nx, gz, fa), BF16),
            vm((ny, gz, fc), BF16),
            vm((nx, gy, fb), BF16),
            vm((nz, rows, fac), F32),
            vm((ny, rows, fb), F32),
            vm((nz, rows, fac), F32),
            vm((ny, rows, fb), F32),
            vm((nz, 1, tokens), F32),
            vm((ny, 1, tokens), F32),
            vm((nx, 1, tokens), F32),
            vm((feat, vocab), BF16),
            pltpu.SemaphoreType.DMA((NEX, 8)),
            pltpu.SemaphoreType.DMA((NEX, 8)),
            pltpu.SemaphoreType.DMA((2,)),
        ],
        compiler_params=pltpu.CompilerParams(collective_id=0, has_side_effects=True, vmem_limit_bytes=60 * 2**20),
        name="head_step",
    )(hidden[0], gain, head[0], labels.reshape(1, tokens))
    return loss, head_grad[None], hidden_grad[None]


def solution(mesh):
    in_specs = (P("member", "fsdp", None), P("member", None), P("member", None, "fsdp"), P())
    out_specs = (P("member", "fsdp"), P("member", None, "fsdp"), P("member", "fsdp", None))
    return jax.shard_map(body, mesh=mesh, in_specs=in_specs, out_specs=out_specs, check_vma=False)
```

time: 2220 us -> 101 us (0.05)
  the two profiles are of different devices: /device:TPU:64 before, /device:TPU:16 now
where the time goes in v1:
time: 101 us
  Pallas kernels  91.3 us (90%)
  local copies, waits for them, and re-layouts  8.95 us (9%)
    pallas_call x1, Pallas kernels, body(): pl.pallas_call(functools.partial(kernel, dims, parts), out_shape=(jax.Sha...  91.3 us
    unnamed x8, local copies, waits for them, and re-layouts  8.95 us

profile of v1, /device:TPU:16, one launch (start us, length us, event | category | flops | bytes accessed | tf_op | source)
XLA Modules:
  0.0 100.9 jit_solution(18422404307443365159)
XLA Ops:
  0.6 3.9 %copy.7 = bf16[1,2048,501]{2,1,0:T(8,128)(2,1)} copy(bf16[1,2048,501]{1,2,0:T(8,128)(2,1)} %param.6) | data formatting | bytes 4104192 | tf_op args[2]
  4.6 91.3 %head_step.1 = (f32[1,2]{1,0:T(1,128)}, bf16[2048,501]{1,0:T(8,128)(2,1)}, bf16[2,2048]{1,0:T(2,128)(2,1)}) custom-call(bf16[2,2048]{1,0:T(2,128)(2,1)} %bitcast.7, f32[1,2048]{1,0:T(1,128)} %gain.1, bf16[2048,501]{1,0:T(8,128)(2,1)} %bitcast.5, s32[1,512]{1,0:T(1,128)} %bitcast.9), custom_call_target="tpu_custom_call" | custom-call | tf_op jit(solution)/shard_map/head_step/pallas_call | solution.py:323
  95.9 0.0 copy-start.1
  95.9 0.0 copy-start
  95.9 3.9 %copy.8 = bf16[1,2048,501]{1,2,0:T(8,128)(2,1)} copy(bf16[1,2048,501]{2,1,0:T(8,128)(2,1)} %bitcast.6) | data formatting | bytes 4104192
  99.8 0.0 copy-done.1
  99.8 0.5 copy.11
  100.3 0.0 copy-done
  100.3 0.6 copy.12
Async XLA Ops:
  95.9 3.9 %copy-start.1 = (f32[1,2]{1,0:T(1,128)S(1)}, f32[1,2]{1,0:T(1,128)}, u32[]{:S(2)}) copy-start(f32[1,2]{1,0:T(1,128)} %get-tuple-element.15) | copy-start | bytes 28
  95.9 4.4 %copy-start = (bf16[2,2048]{1,0:T(2,128)(2,1)S(1)}, bf16[2,2048]{1,0:T(2,128)(2,1)}, u32[]{:S(2)}) copy-start(bf16[2,2048]{1,0:T(2,128)(2,1)} %get-tuple-element.8) | copy-start | bytes 24580

commit v2 on v1

v2 whole, which is shorter than its diff:
```python
import functools
import math

import jax
import jax.numpy as jnp
from jax import lax
from jax.experimental import pallas as pl
from jax.experimental.pallas import tpu as pltpu
from jax.sharding import PartitionSpec as P

EPS = 1e-05
BETA = 0.5
MESH = pl.DeviceIdType.MESH
F32 = jnp.float32
BF16 = jnp.bfloat16
GRID = {256: (8, 4, 8), 8: (2, 2, 2), 16: (4, 2, 2), 32: (8, 2, 2)}
SPLIT = {2048: (640, 512, 896), 384: (128, 128, 128)}

NAMES = [
    "G1Z", "G1Y", "G2A", "G2B", "G2C", "G3C", "SZ", "SY", "SX", "TE", "R1C", "R2A", "R2B", "R2C", "R3Z", "R3Y",
    "QX", "QY", "QZ", "GA", "GB", "RA", "RB",
]
NUM = {name: i for i, name in enumerate(NAMES)}
RINGS = {name: i for i, name in enumerate(["GA", "GB", "RA", "RB"])}
TRACE = False


def dot(a, b, dims):
    return lax.dot_general(a, b, (dims, ((), ())), preferred_element_type=F32)


def kernel(
    dims, parts, hid_in, gain_in, head_hbm, lab_in, loss, hg, hd,
    w, own, z1, y1, asz, asy, na, nc, nb, nbn, lg, tch, stz, sty, stx, ltt, labt,
    dl, dlb, ua, uc, ub, pa, pb, ra, rc, rb, sa2, sc2, sb2, ra2, rc2, rb2,
    s3z, s3y, r3z, r3y, qz, qy, qx, ssem, rsem, gsem, xsem, csem, hid, gain, lab,
):
    ny, nx, nz = dims
    fa, fc, fb = parts
    fac = fa + fc
    rows, feat = hid.shape
    tokens = lab.shape[1]
    vocab = head_hbm.shape[0]
    gz, gy = nz * rows, ny * rows

    f = lax.axis_index("fsdp")
    mem = lax.axis_index("member")
    z = lax.rem(f, nz)
    x = lax.rem(lax.div(f, nz), nx)
    y = lax.div(f, nz * nx)

    def at_z(c):
        return {"fsdp": f - z + c}

    def at_x(c):
        return {"fsdp": f + (c - x) * nz}

    def at_y(c):
        return {"fsdp": f + (c - y) * (nx * nz)}

    def copy(name, src, dst, dev, slot=None, sems=None):
        num = NUM[name]
        arrive = rsem.at[num] if slot is None else (gsem.at[RINGS[name], slot] if sems is None else sems.at[slot])
        return pltpu.make_async_remote_copy(
            src_ref=src, dst_ref=dst, send_sem=ssem.at[num], recv_sem=arrive, device_id=dev, device_id_type=MESH
        )

    sends = []
    near = sorted(range(nx), key=lambda k: min(k, nx - k))
    upward = near[0::2]
    along = [lax.rem(x + k, nx) for k in range(nx)]

    class Exchange:
        def __init__(self, name, n, me, at, src, dst, many):
            self.n, self.me, self.at = n, me, at
            self.make = lambda c: copy(name, src(c), dst, at(c))
            self.all = copy(name, many, many, at(lax.rem(me + 1, n)))
            sends.append(self.all)

        def start(self):
            def step(k, carry):
                self.make(lax.rem(self.me + k, self.n)).start()
                return carry

            lax.fori_loop(1, self.n, step, 0)
            return self

        def arrived(self):
            self.all.wait_recv()

    class Ring:
        def __init__(self, name, n, me, at, many):
            self.name, self.n, self.me, self.at = name, n, me, at
            self.half = n // 2
            self.pending = set()
            sends.append(copy(name, many, many, at(lax.rem(me + 1, n))))

        def other(self, way, steps):
            return lax.rem(self.me + (steps if way == 0 else self.n - steps), self.n)

        def reaches(self, way, d, k):
            return d < self.half or (d == self.half and (k in upward) == (way == 0))

        def slot(self, way, d, k):
            return (way * self.half + d - 1) * nx + k

        def send(self, way, d, k, hops, src, dst):
            copy(self.name, src, dst, self.at(self.other(way, hops)), self.slot(way, d, k)).start()
            self.pending.add((way, d, k))

        def arrived(self, way, d, k, ref):
            self.pending.remove((way, d, k))
            copy(self.name, ref, ref, self.at(self.other(way, 1)), self.slot(way, d, k)).wait_recv()

    scope = []

    def stage(name):
        if TRACE:
            if scope:
                scope.pop().__exit__(None, None, None)
            if name:
                scope.append(jax.named_scope(name))
                scope[0].__enter__()

    stage("greet")
    loads = [
        pltpu.make_async_copy(src, dst, csem.at[i])
        for i, (src, dst) in enumerate([(hid_in, hid), (gain_in, gain), (lab_in, lab), (head_hbm, w)])
    ]
    for load in loads:
        load.start()

    barrier = pltpu.get_barrier_semaphore()

    def greet(dev):
        pl.semaphore_signal(barrier, inc=1, device_id=dev, device_id_type=MESH)

    def greet_all(n, me, at):
        def step(k, carry):
            greet(at(lax.rem(me + k, n)))
            return carry

        lax.fori_loop(1, n, step, 0)

    greet_all(nz, z, at_z)
    greet_all(ny, y, at_y)
    greet_all(nx, x, at_x)
    def at_x_other(c):
        return {"member": 1 - mem, "fsdp": f + (c - x) * nz}

    def greet_other(c, carry):
        greet(at_x_other(c))
        return carry

    lax.fori_loop(0, nx, greet_other, 0)

    loads[0].wait()
    loads[1].wait()
    values = hid[...].astype(F32)
    inverse = lax.rsqrt(jnp.mean(values * values, axis=-1, keepdims=True) + EPS)
    own[...] = (values * inverse * gain[...]).astype(BF16)

    stage("barrier")
    pl.semaphore_wait(barrier, nz - 1 + ny - 1 + nx - 1 + nx)

    stage("g1start")
    g1y = Exchange("G1Y", ny, y, at_y, lambda c: own.at[:, pl.ds(fac, fb)], y1.at[y], y1.at[0:ny - 1]).start()
    g1z = Exchange("G1Z", nz, z, at_z, lambda c: own.at[:, pl.ds(0, fac)], z1.at[z], z1.at[0:nz - 1]).start()

    z1[z] = own[:, :fac]
    y1[y] = own[:, fac:]
    loads[2].wait()
    labt[...] = jnp.broadcast_to(lab[...], (128, tokens)).T
    size = ny * gz
    lr = int(math.log2(rows))
    lz = int(math.log2(nz))
    to = lax.broadcasted_iota(jnp.int32, (size, size), 0)
    frm = lax.broadcasted_iota(jnp.int32, (size, size), 1)
    ty = to >> (lr + lz)
    tz = (to >> lr) & (nz - 1)
    perm = (frm == tz * gy + ty * rows + (to & (rows - 1))).astype(BF16)

    stage("g1y_wait")
    g1y.arrived()
    for s in range(ny):
        asy[s * rows:(s + 1) * rows, :] = y1[s].astype(F32)
    nb[x, z] = asy[...].astype(BF16)

    def to_row(name, which, ref):
        for k in near[1:]:
            copy(name, ref, ref, at_x(along[k]), nx - k, xsem.at[which]).start()

    def from_row(name, which, ref, k):
        copy(name, ref, ref, at_x(along[k]), k, xsem.at[which]).wait_recv()

    def block_a(b, k):
        return na.at[b, along[k]]

    def block_b(b, k):
        return nb.at[along[k], b]

    sends.append(copy("G2A", na.at[0, 0:nx - 1], na.at[0, 0:nx - 1], at_x(along[1])))
    sends.append(copy("G2B", nb.at[0:nx - 1, 0], nb.at[0:nx - 1, 0], at_x(along[1])))
    ring_a = Ring("GA", ny, y, at_y, na.at[0:ny - 1])
    ring_b = Ring("GB", nz, z, at_z, nb.at[:, 0:nz - 1])

    def hand_on(ring, block, late, k, hops=(2, 1)):
        back = 2 * late
        for way in range(2):
            if late:
                if not ring.reaches(way, 3, k):
                    continue
                ring.arrived(way, 2, k, block(ring.other(1 - way, 2), k))
            ref = block(ring.other(1 - way, back) if back else ring.me, k)
            for hop in hops:
                if ring.reaches(way, back + hop, k):
                    ring.send(way, back + hop, k, hop, ref, ref)

    def rest(ring, block):
        for way, d, k in sorted(ring.pending, key=lambda p: (p[1], near.index(p[2]))):
            ring.arrived(way, d, k, block(ring.other(1 - way, d), k))

    to_row("G2B", 1, nb.at[x, z])
    hand_on(ring_b, block_b, 0, 0)
    stage("g1z_wait")
    g1z.arrived()
    for s in range(nz):
        asz[s * rows:(s + 1) * rows, :] = z1[s].astype(F32)
    tile = asz[...].astype(BF16)
    na[y, x] = tile[:, :fa]
    to_row("G2A", 0, na.at[y, x])
    nc[y, x] = tile[:, fa:]
    g2c = Exchange("G2C", ny, y, at_y, lambda c: nc.at[y, x], nc.at[y, x], nc.at[0:ny - 1, 0]).start()
    hand_on(ring_a, block_a, 0, 0)

    def step_b(s, k):
        if s == 0:
            from_row("G2B", 1, nb.at[along[k], z], k)
        hand_on(ring_b, block_b, s, k, (2, 1) if s else (2,))

    def step_a(s, k):
        if s == 0:
            from_row("G2A", 0, na.at[y, along[k]], k)
        hand_on(ring_a, block_a, s, k, (2, 1) if s else (2,))

    def step_1(k):
        hand_on(ring_b, block_b, 0, k, (1,))
        hand_on(ring_a, block_a, 0, k, (1,))

    g3c = Exchange("G3C", nx, x, at_x, lambda c: nc.at[:, x], nc.at[:, x], nc.at[:, 0:nx - 1])

    def turn_c():
        g2c.arrived()
        g3c.start()

    events = [(4.0, "turn_c", turn_c)]
    for k in near[1:]:
        events.append((3.3 + 0.01 * k, f"n{k}", functools.partial(step_1, k)))
    for s in range(2):
        for k in range(nx):
            if (s, k) == (0, 0):
                continue
            when = 3.5 * s + 1.5 * min(k, nx - k) + 0.1 * k
            events.append((when, f"b{s}{k}", functools.partial(step_b, s, k)))
            events.append((when + 0.01, f"a{s}{k}", functools.partial(step_a, s, k)))
    for when, name, event in sorted(events, key=lambda e: e[0]):
        stage(name)
        event()

    stage("load_wait")
    loads[3].wait()
    stage("g3c_wait")
    g3c.arrived()
    stage("dot_c")
    lg[...] = dot(nc[...].reshape(tokens, fc), w[:, fa:fac], ((1,), (1,)))
    stage("g3a_wait")
    rest(ring_a, block_a)
    stage("dot_a")
    lg[...] += dot(na[...].reshape(tokens, fa), w[:, :fa], ((1,), (1,)))
    stage("g3b_wait")
    rest(ring_b, block_b)
    stage("dot_b")
    for s in range(nx):
        swap = dot(perm, nb[s].reshape(size, fb), ((1,), (0,)))
        nbn[:, s] = swap.astype(BF16).reshape(ny, gz, fb)
    lg[...] += dot(nbn[...].reshape(tokens, fb), w[:, fac:], ((1,), (1,)))
    other = copy("TE", lg, tch, {"member": 1 - mem})
    other.start()

    stage("stats")
    logits = lg[...]
    columns = lax.broadcasted_iota(jnp.int32, (tokens, vocab), 1)
    top = jnp.max(logits, axis=-1, keepdims=True)
    total = jnp.sum(jnp.exp(logits - top), axis=-1, keepdims=True)
    lane = lax.broadcasted_iota(jnp.int32, (tokens, 128), 1)
    both = jnp.where(lane == 0, top, total).T
    stz[z] = both[0:2, :]

    def merged(blocks):
        best = functools.reduce(jnp.maximum, [b[0:1, :] for b in blocks])
        return best, functools.reduce(jnp.add, [b[1:2, :] * jnp.exp(b[0:1, :] - best) for b in blocks])

    sz = Exchange("SZ", nz, z, at_z, lambda c: stz.at[z], stz.at[z], stz.at[0:nz - 1]).start()
    stage("sz_wait")
    sz.arrived()
    stage("mergez")
    best, total = merged([stz[s] for s in range(nz)])
    sty[y, 0:1, :] = best
    sty[y, 1:2, :] = total
    sy = Exchange("SY", ny, y, at_y, lambda c: sty.at[y], sty.at[y], sty.at[0:ny - 1]).start()
    stage("sy_wait")
    sy.arrived()
    stage("mergey")
    best, total = merged([sty[s] for s in range(ny)])
    mine = mem * nx + x
    stx[mine, 0:1, :] = best
    stx[mine, 1:2, :] = total

    sx = Exchange("SX", nx, x, at_x, lambda c: stx.at[mine], stx.at[mine], stx.at[0:2 * nx - 1]).start()

    def cross_step(k, carry):
        copy("SX", stx.at[mine], stx.at[mine], at_x_other(lax.rem(x + k, nx))).start()
        return carry

    lax.fori_loop(0, nx, cross_step, 0)
    stage("sx_wait")
    sx.arrived()
    stage("mergex")
    logs = []
    for who in (mem, 1 - mem):
        best, total = merged([stx[who * nx + s] for s in range(nx)])
        logs.append(best + jnp.log(total))
    row = lax.broadcasted_iota(jnp.int32, (128, tokens), 0)
    ltt[...] = jnp.where(row == 0, logs[0], logs[1]).T

    stage("teacher_wait")
    other.wait_recv()
    stage("dlogits")
    local = labt[:, 0:1] - f * vocab
    mask = local == columns
    logits = lg[...]
    log_total = ltt[:, 0:1]
    target = jnp.exp((tch[...] - ltt[:, 1:2]).astype(BF16).astype(F32))
    student = jnp.exp(logits - log_total)
    grad = ((1.0 + BETA) * student - mask.astype(F32) - BETA * target) * (1.0 / tokens)
    dl[...] = grad.astype(BF16).reshape(ny, nx, gz, vocab)
    part = jnp.sum(BETA * target * (log_total - logits) - jnp.where(mask, logits, 0.0), axis=-1, keepdims=True)
    qx[x] = jnp.broadcast_to(part, (tokens, 128)).T[0:1, :]
    q1 = Exchange("QX", nx, x, at_x, lambda c: qx.at[x], qx.at[x], qx.at[0:nx - 1]).start()

    stage("up_b")
    for s in range(nx):
        swap = dot(perm, dl[:, s].reshape(size, vocab), ((0,), (0,)))
        dlb[s] = swap.astype(BF16).reshape(nz, gy, vocab)
    back_b = Ring("RB", nz, z, at_z, pb.at[0:(nz - 1) * nx])
    back_a = Ring("RA", ny, y, at_y, pa.at[0:(ny - 1) * nx])

    def own_a(b, k):
        return ua[b, along[k]]

    def own_b(b, k):
        return ub[along[k], b]

    def send_on(ring, put, got, way, d, k, hops, acc):
        here = ring.slot(way, d, k)
        put[here] = acc.astype(BF16)
        ring.send(way, d, k, hops, put.at[here], got.at[here])

    def taken(ring, got, way, d, k, acc):
        if (way, d, k) in ring.pending:
            here = ring.slot(way, d, k)
            ring.arrived(way, d, k, got.at[here])
            acc = acc + got[here].astype(F32)
        return acc

    def far_off(ring, own_of, put, got, k):
        for d in (4, 3):
            for way in range(2):
                if ring.reaches(way, d, k):
                    send_on(ring, put, got, way, d, k, d - 2, own_of(ring.other(way, d), k))

    def next_to(ring, own_of, put, got, k):
        for way in range(2):
            if ring.reaches(way, 1, k):
                send_on(ring, put, got, way, 1, k, 1, own_of(ring.other(way, 1), k))

    def two_off(ring, own_of, put, got, k):
        for way in range(2):
            if ring.reaches(way, 2, k):
                acc = own_of(ring.other(way, 2), k)
                for d in (3, 4):
                    acc = taken(ring, got, way, d, k, acc)
                send_on(ring, put, got, way, 2, k, 2, acc)

    def ended(ring, own_of, got, k):
        acc = own_of(ring.me, k)
        for d in (1, 2):
            for way in range(2):
                acc = taken(ring, got, way, d, k, acc)
        return acc

    far = near[::-1]
    args_a = back_a, own_a, pa, ra
    args_b = back_b, own_b, pb, rb

    ub[...] = dot(dlb[...].reshape(tokens, vocab), w[:, fac:], ((1,), (0,))).reshape(ub.shape)
    for k in far:
        far_off(*args_b, k)
    stage("up_a")
    whole = dl[...].reshape(tokens, vocab)
    ua[...] = dot(whole, w[:, :fa], ((1,), (0,))).reshape(ua.shape)
    for k in far:
        far_off(*args_a, k)
    stage("up_c")
    uc[...] = dot(whole, w[:, fa:fac], ((1,), (0,))).astype(BF16).reshape(uc.shape)
    r1c = Exchange("R1C", nx, x, at_x, lambda c: uc.at[:, c], rc.at[x], rc.at[0:nx - 1]).start()
    stage("fresh1")

    stage("hg")
    flat = whole.T
    hg[:, :fa] = dot(flat, na[...].reshape(tokens, fa), ((1,), (0,))).astype(BF16)
    hg[:, fa:fac] = dot(flat, nc[...].reshape(tokens, fc), ((1,), (0,))).astype(BF16)
    hg[:, fac:] = dot(flat, nbn[...].reshape(tokens, fb), ((1,), (0,))).astype(BF16)

    def summed(mine, arrived, me, n, index):
        acc = mine.astype(F32)
        for k in range(1, n):
            acc = acc + arrived[(lax.rem(me + k, n),) + index].astype(F32)
        return acc

    q2 = Exchange("QY", ny, y, at_y, lambda c: qy.at[y], qy.at[y], qy.at[0:ny - 1])
    q3 = Exchange("QZ", nz, z, at_z, lambda c: qz.at[z], qz.at[z], qz.at[0:nz - 1])
    r2a = copy("R2A", ra2.at[0:nx - 1], ra2.at[0:nx - 1], at_x(along[1]))
    r2b = copy("R2B", rb2.at[0:nx - 1], rb2.at[0:nx - 1], at_x(along[1]))
    r2c = Exchange("R2C", ny, y, at_y, lambda c: sc2.at[c], rc2.at[y], rc2.at[0:ny - 1])
    sends.extend([r2a, r2b])

    def turn_q2():
        q1.arrived()
        qy[y] = functools.reduce(jnp.add, [qx[s] for s in range(nx)])
        q2.start()

    def turn_q3():
        q2.arrived()
        qz[z] = functools.reduce(jnp.add, [qy[s] for s in range(ny)])
        q3.start()

    def turn_rc():
        r1c.arrived()
        for s in range(ny):
            sc2[s] = summed(uc[s, x], rc, x, nx, (s,)).astype(BF16)
        r2c.start()

    def row_b(k):
        sb2[k] = ended(back_b, own_b, rb, k).astype(BF16)
        if k:
            copy("R2B", sb2.at[k], rb2.at[x], at_x(along[k])).start()

    def row_a(k):
        sa2[k] = ended(back_a, own_a, ra, k).astype(BF16)
        if k:
            copy("R2A", sa2.at[k], ra2.at[x], at_x(along[k])).start()

    events = [(4.5, "turn_q2", turn_q2), (9.1, "turn_q3", turn_q3), (7.5, "turn_rc", turn_rc)]
    for i, k in enumerate(far):
        when = 3.5 + 0.7 * i
        events.append((when, f"rb{k}", functools.partial(two_off, *args_b, k)))
        events.append((when + 0.01, f"ra{k}", functools.partial(two_off, *args_a, k)))
        events.append((when + 0.02, f"nb{k}", functools.partial(next_to, *args_b, k)))
        events.append((when + 0.03, f"na{k}", functools.partial(next_to, *args_a, k)))
        when = 9.5 + 0.7 * i
        events.append((when, f"rowb{k}", functools.partial(row_b, k)))
        events.append((when + 0.01, f"rowa{k}", functools.partial(row_a, k)))
    for when, name, event in sorted(events, key=lambda e: e[0]):
        stage(name)
        event()

    stage("r2b_wait")
    r2b.wait_recv()
    stage("sum2b")
    asy[...] = summed(sb2[0], rb2, x, nx, ())
    for s in range(ny):
        s3y[s] = asy[s * rows:(s + 1) * rows, :]
    r4 = Exchange("R3Y", ny, y, at_y, lambda c: s3y.at[c], r3y.at[y], r3y.at[0:ny - 1]).start()
    stage("r2c_wait")
    r2c.arrived()
    asz[:, fa:] = summed(sc2[y], rc2, y, ny, ())
    stage("r2a_wait")
    r2a.wait_recv()
    stage("sum2")
    asz[:, :fa] = summed(sa2[0], ra2, x, nx, ())
    for s in range(nz):
        s3z[s] = asz[s * rows:(s + 1) * rows, :]
    r3 = Exchange("R3Z", nz, z, at_z, lambda c: s3z.at[c], r3z.at[z], r3z.at[0:nz - 1]).start()

    q3.arrived()
    stage("loss")
    losses = functools.reduce(jnp.add, [qz[s] for s in range(nz)]) + logs[0]
    spot = lax.broadcasted_iota(jnp.int32, (1, tokens), 1)
    for i in range(rows):
        loss[:, i:i + 1] = jnp.sum(jnp.where(spot == f * rows + i, losses, 0.0), axis=-1, keepdims=True)

    stage("r3_wait")
    r3.arrived()
    r4.arrived()
    stage("final")
    upstream = jnp.concatenate([summed(s3z[z], r3z, z, nz, ()), summed(s3y[y], r3y, y, ny, ())], axis=-1)
    scaled = gain[...] * upstream
    inner = jnp.mean(scaled * values, axis=-1, keepdims=True)
    hd[...] = (inverse * scaled - values * (inverse * inverse * inverse) * inner).astype(BF16)

    stage("sent_wait")
    for all_sent in sends:
        all_sent.wait_send()
    other.wait_send()
    stage(None)


def finish_kernel(*refs):
    half = len(refs) // 2
    copies = [pltpu.make_async_copy(a, b, refs[-1].at[i]) for i, (a, b) in enumerate(zip(refs[:half], refs[half:-1]))]
    for copy in copies:
        copy.start()
    for copy in copies:
        copy.wait()


def finish(*arrays):
    n = len(arrays)
    return pl.pallas_call(
        finish_kernel,
        out_shape=tuple(jax.ShapeDtypeStruct(a.shape, a.dtype) for a in arrays),
        in_specs=[pl.BlockSpec(memory_space=pltpu.VMEM)] * n,
        out_specs=[pl.BlockSpec(memory_space=pl.ANY)] * n,
        scratch_shapes=[pltpu.SemaphoreType.DMA((n,))],
        compiler_params=pltpu.CompilerParams(vmem_limit_bytes=2**20),
        name="finish",
    )(*arrays)


def body(hidden, gain, head, labels):
    rows, feat = hidden.shape[1:]
    vocab = head.shape[2]
    tokens = labels.shape[0]
    ny, nx, nz = dims = GRID[tokens // rows]
    fa, fc, fb = parts = SPLIT[feat]
    fac = fa + fc
    gz, gy = nz * rows, ny * rows
    vm = pltpu.VMEM
    loss, head_grad, hidden_grad = pl.pallas_call(
        functools.partial(kernel, dims, parts),
        out_shape=(
            vm((1, rows), F32),
            vm((vocab, feat), BF16),
            vm((rows, feat), BF16),
        ),
        in_specs=[pl.BlockSpec(memory_space=pltpu.HBM)] * 4,
        out_specs=[pl.BlockSpec(memory_space=vm)] * 3,
        scratch_shapes=[
            vm((vocab, feat), BF16),
            vm((rows, feat), BF16),
            vm((nz, rows, fac), BF16),
            vm((ny, rows, fb), BF16),
            vm((gz, fac), F32),
            vm((gy, fb), F32),
            vm((ny, nx, gz, fa), BF16),
            vm((ny, nx, gz, fc), BF16),
            vm((nx, nz, gy, fb), BF16),
            vm((ny, nx, gz, fb), BF16),
            vm((tokens, vocab), F32),
            vm((tokens, vocab), F32),
            vm((nz, 2, tokens), F32),
            vm((ny, 2, tokens), F32),
            vm((2 * nx, 2, tokens), F32),
            vm((tokens, 128), F32),
            vm((tokens, 128), jnp.int32),
            vm((ny, nx, gz, vocab), BF16),
            vm((nx, nz, gy, vocab), BF16),
            vm((ny, nx, gz, fa), F32),
            vm((ny, nx, gz, fc), BF16),
            vm((nx, nz, gy, fb), F32),
            vm((ny * nx, gz, fa), BF16),
            vm((nz * nx, gy, fb), BF16),
            vm((ny * nx, gz, fa), BF16),
            vm((nx, ny, gz, fc), BF16),
            vm((nz * nx, gy, fb), BF16),
            vm((nx, gz, fa), BF16),
            vm((ny, gz, fc), BF16),
            vm((nx, gy, fb), BF16),
            vm((nx, gz, fa), BF16),
            vm((ny, gz, fc), BF16),
            vm((nx, gy, fb), BF16),
            vm((nz, rows, fac), F32),
            vm((ny, rows, fb), F32),
            vm((nz, rows, fac), F32),
            vm((ny, rows, fb), F32),
            vm((nz, 1, tokens), F32),
            vm((ny, 1, tokens), F32),
            vm((nx, 1, tokens), F32),
            pltpu.SemaphoreType.DMA((len(NUM),)),
            pltpu.SemaphoreType.DMA((len(NUM),)),
            pltpu.SemaphoreType.DMA((len(RINGS), max(ny, nz) * nx)),
            pltpu.SemaphoreType.DMA((2, nx)),
            pltpu.SemaphoreType.DMA((4,)),
            vm((rows, feat), BF16),
            vm((1, feat), F32),
            vm((1, tokens), jnp.int32),
        ],
        compiler_params=pltpu.CompilerParams(collective_id=0, has_side_effects=True, vmem_limit_bytes=123 * 2**19),
        name="head_step",
    )(hidden[0], gain, head[0].T, labels.reshape(1, tokens))
    loss, head_grad, hidden_grad = finish(loss, head_grad, hidden_grad)
    return loss, head_grad.T[None], hidden_grad[None]


def solution(mesh):
    in_specs = (P("member", "fsdp", None), P("member", None), P("member", None, "fsdp"), P())
    out_specs = (P("member", "fsdp"), P("member", None, "fsdp"), P("member", "fsdp", None))
    return jax.shard_map(body, mesh=mesh, in_specs=in_specs, out_specs=out_specs, check_vma=False)
```

time: 101 us -> 75.6 us (0.75)
  the two profiles are of different devices: /device:TPU:16 before, /device:TPU:2 now
where the time goes in v2:
time: 75.6 us; the launch traced here: 75.5 us
  Pallas kernels  74.8 us (99%)
    pallas_call x1, Pallas kernels, body(): pl.pallas_call(functools.partial(kernel, dims, parts), out_shape=(vm((1,...  73.5 us

profile of v2, /device:TPU:2, one launch (start us, length us, event | category | flops | bytes accessed | tf_op | source)
XLA Modules:
  0.0 75.5 jit_solution(16205105596016182218)
XLA Ops:
  0.6 73.5 %head_step.1 = (f32[1,2]{1,0:T(1,128)S(1)}, bf16[501,2048]{1,0:T(8,128)(2,1)S(1)}, bf16[2,2048]{1,0:T(2,128)(2,1)S(1)}) custom-call(bf16[2,2048]{1,0:T(2,128)(2,1)} %bitcast.10, f32[1,2048]{1,0:T(1,128)} %gain_in.1, bf16[501,2048]{1,0:T(8,128)(2,1)} %bitcast.9, s32[1,512]{1,0:T(1,128)} %bitcast.11), custom_call_target="tpu_custom_call" | custom-call | tf_op jit(solution)/shard_map/head_step/pallas_call | solution.py:550
  74.1 1.3 %finish.1 = (f32[1,2]{1,0:T(1,128)}, bf16[501,2048]{1,0:T(8,128)(2,1)}, bf16[2,2048]{1,0:T(2,128)(2,1)}) custom-call(f32[1,2]{1,0:T(1,128)S(1)} %get-tuple-element.9.refs_0_, bf16[501,2048]{1,0:T(8,128)(2,1)S(1)} %get-tuple-element.10.refs_1_, bf16[2,2048]{1,0:T(2,128)(2,1)S(1)} %get-tuple-element.11.refs_2_), custom_call_target="tpu_custom_call" | custom-call | tf_op jit(solution)/shard_map/finish/pallas_call | solution.py:530

commit v3 on v2

--- a/solution.py
+++ b/solution.py
@@ -21,7 +21,7 @@
     "QX", "QY", "QZ", "GA", "GB", "RA", "RB",
 ]
 NUM = {name: i for i, name in enumerate(NAMES)}
-RINGS = {name: i for i, name in enumerate(["GA", "GB", "RA", "RB"])}
+RINGS = {"GA": 0, "GB": 1, "RA": 0, "RB": 1}
 TRACE = False
 
 
@@ -170,7 +170,7 @@
     z1[z] = own[:, :fac]
     y1[y] = own[:, fac:]
     loads[2].wait()
-    labt[...] = jnp.broadcast_to(lab[...], (128, tokens)).T
+    labt[...] = jnp.broadcast_to(lab[...], (128, tokens)).T.reshape(labt.shape)
     size = ny * gz
     lr = int(math.log2(rows))
     lz = int(math.log2(nz))
@@ -216,8 +216,8 @@
                 if ring.reaches(way, back + hop, k):
                     ring.send(way, back + hop, k, hop, ref, ref)
 
-    def rest(ring, block):
-        for way, d, k in sorted(ring.pending, key=lambda p: (p[1], near.index(p[2]))):
+    def rest(ring, block, k):
+        for way, d, _ in sorted(p for p in ring.pending if p[2] == k):
             ring.arrived(way, d, k, block(ring.other(1 - way, d), k))
 
     to_row("G2B", 1, nb.at[x, z])
@@ -271,30 +271,34 @@
     loads[3].wait()
     stage("g3c_wait")
     g3c.arrived()
-    stage("dot_c")
-    lg[...] = dot(nc[...].reshape(tokens, fc), w[:, fa:fac], ((1,), (1,)))
-    stage("g3a_wait")
-    rest(ring_a, block_a)
-    stage("dot_a")
-    lg[...] += dot(na[...].reshape(tokens, fa), w[:, :fa], ((1,), (1,)))
-    stage("g3b_wait")
-    rest(ring_b, block_b)
-    stage("dot_b")
-    for s in range(nx):
-        swap = dot(perm, nb[s].reshape(size, fb), ((1,), (0,)))
-        nbn[:, s] = swap.astype(BF16).reshape(ny, gz, fb)
-    lg[...] += dot(nbn[...].reshape(tokens, fb), w[:, fac:], ((1,), (1,)))
-    other = copy("TE", lg, tch, {"member": 1 - mem})
-    other.start()
-
-    stage("stats")
-    logits = lg[...]
-    columns = lax.broadcasted_iota(jnp.int32, (tokens, vocab), 1)
-    top = jnp.max(logits, axis=-1, keepdims=True)
-    total = jnp.sum(jnp.exp(logits - top), axis=-1, keepdims=True)
-    lane = lax.broadcasted_iota(jnp.int32, (tokens, 128), 1)
-    both = jnp.where(lane == 0, top, total).T
-    stz[z] = both[0:2, :]
+
+    def joined(parts):
+        return jnp.concatenate([p.reshape(size, p.shape[-1]) for p in parts], axis=0)
+
+    def lanes(k):
+        return pl.ds(pl.multiple_of(along[k] * size, size), size)
+
+    for group in (near[:nx // 2], near[nx // 2:]):
+        for k in group:
+            stage(f"rest{k}")
+            rest(ring_b, block_b, k)
+            rest(ring_a, block_a, k)
+        stage(f"logits{group[0]}")
+        for k in group:
+            swap = dot(perm, nb[along[k]].reshape(size, fb), ((1,), (0,)))
+            nbn[:, along[k]] = swap.astype(BF16).reshape(ny, gz, fb)
+        logits = (
+            dot(joined([nc[:, along[k]] for k in group]), w[:, fa:fac], ((1,), (1,)))
+            + dot(joined([na[:, along[k]] for k in group]), w[:, :fa], ((1,), (1,)))
+            + dot(joined([nbn[:, along[k]] for k in group]), w[:, fac:], ((1,), (1,)))
+        )
+        top = jnp.max(logits, axis=-1, keepdims=True)
+        total = jnp.sum(jnp.exp(logits - top), axis=-1, keepdims=True)
+        lane = lax.broadcasted_iota(jnp.int32, (logits.shape[0], 128), 1)
+        both = jnp.where(lane == 0, top, total).T
+        for i, k in enumerate(group):
+            lg[along[k]] = logits[i * size:(i + 1) * size, :]
+            stz[z, :, lanes(k)] = both[0:2, i * size:(i + 1) * size]
 
     def merged(blocks):
         best = functools.reduce(jnp.maximum, [b[0:1, :] for b in blocks])
@@ -302,6 +306,8 @@
 
     sz = Exchange("SZ", nz, z, at_z, lambda c: stz.at[z], stz.at[z], stz.at[0:nz - 1]).start()
     stage("sz_wait")
+    other = copy("TE", lg, tch, {"member": 1 - mem})
+    other.start()
     sz.arrived()
     stage("mergez")
     best, total = merged([stz[s] for s in range(nz)])
@@ -331,27 +337,29 @@
         best, total = merged([stx[who * nx + s] for s in range(nx)])
         logs.append(best + jnp.log(total))
     row = lax.broadcasted_iota(jnp.int32, (128, tokens), 0)
-    ltt[...] = jnp.where(row == 0, logs[0], logs[1]).T
+    ltt[...] = jnp.where(row == 0, logs[0], logs[1]).T.reshape(ltt.shape)
 
     stage("teacher_wait")
     other.wait_recv()
     stage("dlogits")
-    local = labt[:, 0:1] - f * vocab
-    mask = local == columns
-    logits = lg[...]
-    log_total = ltt[:, 0:1]
-    target = jnp.exp((tch[...] - ltt[:, 1:2]).astype(BF16).astype(F32))
-    student = jnp.exp(logits - log_total)
-    grad = ((1.0 + BETA) * student - mask.astype(F32) - BETA * target) * (1.0 / tokens)
-    dl[...] = grad.astype(BF16).reshape(ny, nx, gz, vocab)
-    part = jnp.sum(BETA * target * (log_total - logits) - jnp.where(mask, logits, 0.0), axis=-1, keepdims=True)
-    qx[x] = jnp.broadcast_to(part, (tokens, 128)).T[0:1, :]
-    q1 = Exchange("QX", nx, x, at_x, lambda c: qx.at[x], qx.at[x], qx.at[0:nx - 1]).start()
-
-    stage("up_b")
-    for s in range(nx):
-        swap = dot(perm, dl[:, s].reshape(size, vocab), ((0,), (0,)))
-        dlb[s] = swap.astype(BF16).reshape(nz, gy, vocab)
+    columns = lax.broadcasted_iota(jnp.int32, (size, vocab), 1)
+
+    def logits_back(k):
+        local = labt[:, along[k]].reshape(size, 128)[:, 0:1] - f * vocab
+        mask = local == columns
+        logits = lg[along[k]]
+        log_total = ltt[along[k]][:, 0:1]
+        target = jnp.exp((tch[along[k]] - ltt[along[k]][:, 1:2]).astype(BF16).astype(F32))
+        student = jnp.exp(logits - log_total)
+        grad = ((1.0 + BETA) * student - mask.astype(F32) - BETA * target) * (1.0 / tokens)
+        grad = grad.astype(BF16)
+        dl[:, along[k]] = grad.reshape(ny, gz, vocab)
+        dlb[along[k]] = dot(perm, grad, ((0,), (0,))).astype(BF16).reshape(nz, gy, vocab)
+        part = jnp.sum(
+            BETA * target * (log_total - logits) - jnp.where(mask, logits, 0.0), axis=-1, keepdims=True
+        )
+        qx[x, :, lanes(k)] = jnp.broadcast_to(part, (size, 128)).T[0:1, :]
+
     back_b = Ring("RB", nz, z, at_z, pb.at[0:(nz - 1) * nx])
     back_a = Ring("RA", ny, y, at_y, pa.at[0:(ny - 1) * nx])
 
@@ -403,15 +411,23 @@
     args_a = back_a, own_a, pa, ra
     args_b = back_b, own_b, pb, rb
 
-    ub[...] = dot(dlb[...].reshape(tokens, vocab), w[:, fac:], ((1,), (0,))).reshape(ub.shape)
-    for k in far:
-        far_off(*args_b, k)
-    stage("up_a")
+    for group in (far[:nx // 2], far[nx // 2:]):
+        stage(f"dlogits{group[0]}")
+        for k in group:
+            logits_back(k)
+        stage(f"up_b{group[0]}")
+        rise = dot(joined([dlb[along[k]] for k in group]), w[:, fac:], ((1,), (0,)))
+        for i, k in enumerate(group):
+            ub[along[k]] = rise[i * size:(i + 1) * size, :].reshape(nz, gy, fb)
+            far_off(*args_b, k)
+        stage(f"up_a{group[0]}")
+        rise = dot(joined([dl[:, along[k]] for k in group]), w[:, :fa], ((1,), (0,)))
+        for i, k in enumerate(group):
+            ua[:, along[k]] = rise[i * size:(i + 1) * size, :].reshape(ny, gz, fa)
+            far_off(*args_a, k)
+    stage("up_c")
+    q1 = Exchange("QX", nx, x, at_x, lambda c: qx.at[x], qx.at[x], qx.at[0:nx - 1]).start()
     whole = dl[...].reshape(tokens, vocab)
-    ua[...] = dot(whole, w[:, :fa], ((1,), (0,))).reshape(ua.shape)
-    for k in far:
-        far_off(*args_a, k)
-    stage("up_c")
     uc[...] = dot(whole, w[:, fa:fac], ((1,), (0,))).astype(BF16).reshape(uc.shape)
     r1c = Exchange("R1C", nx, x, at_x, lambda c: uc.at[:, c], rc.at[x], rc.at[0:nx - 1]).start()
     stage("fresh1")
@@ -498,7 +514,7 @@
     losses = functools.reduce(jnp.add, [qz[s] for s in range(nz)]) + logs[0]
     spot = lax.broadcasted_iota(jnp.int32, (1, tokens), 1)
     for i in range(rows):
-        loss[:, i:i + 1] = jnp.sum(jnp.where(spot == f * rows + i, losses, 0.0), axis=-1, keepdims=True)
+        loss[:, i:i + 1] = jnp.sum(jnp.where(spot == x * size + y * gz + z * rows + i, losses, 0.0), axis=-1, keepdims=True)
 
     stage("r3_wait")
     r3.arrived()
@@ -567,13 +583,13 @@
             vm((ny, nx, gz, fc), BF16),
             vm((nx, nz, gy, fb), BF16),
             vm((ny, nx, gz, fb), BF16),
-            vm((tokens, vocab), F32),
-            vm((tokens, vocab), F32),
+            vm((nx, ny * gz, vocab), F32),
+            vm((nx, ny * gz, vocab), F32),
             vm((nz, 2, tokens), F32),
             vm((ny, 2, tokens), F32),
             vm((2 * nx, 2, tokens), F32),
-            vm((tokens, 128), F32),
-            vm((tokens, 128), jnp.int32),
+            vm((nx, ny * gz, 128), F32),
+            vm((ny, nx, gz, 128), jnp.int32),
             vm((ny, nx, gz, vocab), BF16),
             vm((nx, nz, gy, vocab), BF16),
             vm((ny, nx, gz, fa), F32),
@@ -599,7 +615,7 @@
             vm((nx, 1, tokens), F32),
             pltpu.SemaphoreType.DMA((len(NUM),)),
             pltpu.SemaphoreType.DMA((len(NUM),)),
-            pltpu.SemaphoreType.DMA((len(RINGS), max(ny, nz) * nx)),
+            pltpu.SemaphoreType.DMA((2, max(ny, nz) * nx)),
             pltpu.SemaphoreType.DMA((2, nx)),
             pltpu.SemaphoreType.DMA((4,)),
             vm((rows, feat), BF16),

time: 75.6 us -> 74 us (0.979)
  Pallas kernels: 74.8 us -> 73.2 us
    pallas_call x1, Pallas kernels: 73.5 us -> 71.9 us  [body(): pl.pallas_call(functools.partial(kernel, dims, parts), out_shape=(vm((1,...]
where the time goes in v3:
time: 74 us; the launch traced here: 73.9 us
  Pallas kernels  73.2 us (99%)
    pallas_call x1, Pallas kernels, body(): pl.pallas_call(functools.partial(kernel, dims, parts), out_shape=(vm((1,...  71.9 us

profile of v3, /device:TPU:2, one launch (start us, length us, event | category | flops | bytes accessed | tf_op | source)
XLA Modules:
  0.0 73.9 jit_solution(10124657010157183707)
XLA Ops:
  0.6 71.9 %head_step.1 = (f32[1,2]{1,0:T(1,128)S(1)}, bf16[501,2048]{1,0:T(8,128)(2,1)S(1)}, bf16[2,2048]{1,0:T(2,128)(2,1)S(1)}) custom-call(bf16[2,2048]{1,0:T(2,128)(2,1)} %bitcast.10, f32[1,2048]{1,0:T(1,128)} %gain_in.1, bf16[501,2048]{1,0:T(8,128)(2,1)} %bitcast.9, s32[1,512]{1,0:T(1,128)} %bitcast.11), custom_call_target="tpu_custom_call" | custom-call | tf_op jit(solution)/shard_map/head_step/pallas_call | solution.py:566
  72.5 1.3 %finish.1 = (f32[1,2]{1,0:T(1,128)}, bf16[501,2048]{1,0:T(8,128)(2,1)}, bf16[2,2048]{1,0:T(2,128)(2,1)}) custom-call(f32[1,2]{1,0:T(1,128)S(1)} %get-tuple-element.9.refs_0_, bf16[501,2048]{1,0:T(8,128)(2,1)S(1)} %get-tuple-element.10.refs_1_, bf16[2,2048]{1,0:T(2,128)(2,1)S(1)} %get-tuple-element.11.refs_2_), custom_call_target="tpu_custom_call" | custom-call | tf_op jit(solution)/shard_map/finish/pallas_call | solution.py:546

commit v4 on v3

--- a/solution.py
+++ b/solution.py
@@ -27,6 +27,11 @@
 
 def dot(a, b, dims):
     return lax.dot_general(a, b, (dims, ((), ())), preferred_element_type=F32)
+
+
+def farthest(n, j):
+    odd = lax.rem(j, 2)
+    return n // 2 + lax.div(j + 1, 2) * (1 - 2 * odd)
 
 
 def kernel(
@@ -78,11 +83,11 @@
             sends.append(self.all)
 
         def start(self):
-            def step(k, carry):
-                self.make(lax.rem(self.me + k, self.n)).start()
+            def step(j, carry):
+                self.make(lax.rem(self.me + farthest(self.n, j), self.n)).start()
                 return carry
 
-            lax.fori_loop(1, self.n, step, 0)
+            lax.fori_loop(0, self.n - 1, step, 0)
             return self
 
         def arrived(self):
@@ -136,11 +141,11 @@
         pl.semaphore_signal(barrier, inc=1, device_id=dev, device_id_type=MESH)
 
     def greet_all(n, me, at):
-        def step(k, carry):
-            greet(at(lax.rem(me + k, n)))
+        def step(j, carry):
+            greet(at(lax.rem(me + farthest(n, j), n)))
             return carry
 
-        lax.fori_loop(1, n, step, 0)
+        lax.fori_loop(0, n - 1, step, 0)
 
     greet_all(nz, z, at_z)
     greet_all(ny, y, at_y)

time: 74 us -> 73.1 us (0.988)
  the two profiles are of different devices: /device:TPU:2 before, /device:TPU:8 now
where the time goes in v4:
time: 73.1 us; the launch traced here: 73 us
  Pallas kernels  72.3 us (99%)
    pallas_call x1, Pallas kernels, body(): pl.pallas_call(functools.partial(kernel, dims, parts), out_shape=(vm((1,...  71 us

profile of v4, /device:TPU:8, one launch (start us, length us, event | category | flops | bytes accessed | tf_op | source)
XLA Modules:
  0.0 73.0 jit_solution(5370171288065978925)
XLA Ops:
  0.6 71.0 %head_step.1 = (f32[1,2]{1,0:T(1,128)S(1)}, bf16[501,2048]{1,0:T(8,128)(2,1)S(1)}, bf16[2,2048]{1,0:T(2,128)(2,1)S(1)}) custom-call(bf16[2,2048]{1,0:T(2,128)(2,1)} %bitcast.10, f32[1,2048]{1,0:T(1,128)} %gain_in.1, bf16[501,2048]{1,0:T(8,128)(2,1)} %bitcast.9, s32[1,512]{1,0:T(1,128)} %bitcast.11), custom_call_target="tpu_custom_call" | custom-call | tf_op jit(solution)/shard_map/head_step/pallas_call | solution.py:571
  71.6 1.3 %finish.1 = (f32[1,2]{1,0:T(1,128)}, bf16[501,2048]{1,0:T(8,128)(2,1)}, bf16[2,2048]{1,0:T(2,128)(2,1)}) custom-call(f32[1,2]{1,0:T(1,128)S(1)} %get-tuple-element.9.refs_0_, bf16[501,2048]{1,0:T(8,128)(2,1)S(1)} %get-tuple-element.10.refs_1_, bf16[2,2048]{1,0:T(2,128)(2,1)S(1)} %get-tuple-element.11.refs_2_), custom_call_target="tpu_custom_call" | custom-call | tf_op jit(solution)/shard_map/finish/pallas_call | solution.py:551
